TPU v7x, 32 devices: a whole 2x2x4 slice. The times are simulated.
32 devices in a mesh: dp: 8 (over z, x), ctx: 4 (over y, core).
Axes of the slice: x: 2, y: 2, z: 4, core: 2. Of those that a mesh axis runs over, the one named last changes fastest.
Arguments:
- tokens: bfloat16 [32, 2560, 1280], P('dp', 'ctx'), may hold values from -64 to 64
- router: bfloat16 [1280, 64], replicated, may hold values from -1 to 1
- expert_up: bfloat16 [32, 1280, 2560], P(('dp', 'ctx')), may hold values from -0.5 to 0.5
- expert_down: bfloat16 [32, 2560, 1280], P(('dp', 'ctx')), may hold values from -0.25 to 0.25
Outputs:
- mixed: bfloat16 [32, 2560, 1280], P('dp', 'ctx')
All inputs are finite; a program needn't handle non-finite values.
Results may differ from a plain program's by a relative error of at most 0.015.
Values may be sent and summed in bfloat16 or wider, within the bound.
A program may use at most 128 MiB of HBM per device.

v0:
```python
import jax
import jax.numpy as jnp
from jax import lax
from jax.sharding import PartitionSpec as P


def merged(x, axis, combine):
    everything = jax.tree.map(lambda part: lax.all_gather(part, axis), x)
    initial = jax.tree.map(lambda part: part[0], everything)

    def step(k, so_far):
        return combine(so_far, jax.tree.map(lambda part: part[k], everything))

    return lax.fori_loop(1, lax.axis_size(axis), step, initial)


def merge_stats(earlier, later):
    highest = jnp.maximum(earlier[0], later[0])
    return (
        highest,
        earlier[1] * jnp.exp(earlier[0] - highest) + later[1] * jnp.exp(later[0] - highest),
    )


def expert_rows(grouped, up_matrix, down_matrix):
    feature = grouped.shape[-1]
    flat = grouped.reshape(-1, feature)
    hidden = jax.nn.gelu(
        jnp.dot(flat, up_matrix, preferred_element_type=jnp.float32), approximate=False
    ).astype(jnp.bfloat16)
    produced = jnp.dot(hidden, down_matrix, preferred_element_type=jnp.float32).astype(jnp.bfloat16)
    return produced.reshape(grouped.shape)


def shards(tokens, router, expert_up, expert_down):
    clip_dev, tok_dev, feature = tokens.shape
    dp_size = lax.axis_size("dp")
    ctx_size = lax.axis_size("ctx")
    slot_total = router.shape[1]
    per_expert = slot_total // (dp_size * ctx_size)
    ordered = (
        router.reshape(feature, dp_size, ctx_size, per_expert)
        .transpose(0, 2, 1, 3)
        .reshape(feature, slot_total)
    )
    logits = jnp.einsum("ctd,dj->ctj", tokens, ordered, preferred_element_type=jnp.float32)
    local_max = jnp.max(logits, axis=1)
    exponent = jnp.exp(logits - local_max[:, None, :])
    column_max, column_sum = merged((local_max, jnp.sum(exponent, axis=1)), "ctx", merge_stats)
    exponent = exponent * jnp.exp(local_max - column_max)[:, None, :]
    dispatch = (exponent / column_sum[:, None, :]).astype(jnp.bfloat16)
    row_max = jnp.max(logits, axis=2)
    row_exp = jnp.exp(logits - row_max[:, :, None])
    combine = (row_exp / jnp.sum(row_exp, axis=2)[:, :, None]).astype(jnp.bfloat16)
    up_matrix = expert_up[0]
    down_matrix = expert_down[0]
    split_dispatch = dispatch.reshape(clip_dev, tok_dev, ctx_size, dp_size, per_expert)
    partial_value = jnp.einsum(
        "ctabs,ctd->cbasd", split_dispatch, tokens, preferred_element_type=jnp.float32
    ).astype(jnp.bfloat16)
    grouped = partial_value.reshape(clip_dev, dp_size * ctx_size, per_expert, feature)
    received = lax.all_to_all(grouped, ("dp", "ctx"), split_axis=1, concat_axis=1, tiled=True)
    amount = received.shape[0]
    blocks = received.astype(jnp.float32).reshape(amount, dp_size, ctx_size, per_expert, feature)
    results = expert_rows(jnp.sum(blocks, axis=2).astype(jnp.bfloat16), up_matrix, down_matrix)
    returned = lax.all_to_all(results, "dp", split_axis=1, concat_axis=1, tiled=True)
    returned = returned.reshape(clip_dev, dp_size * per_expert, feature)
    mixed = jnp.einsum(
        "ctj,cjd->ctd",
        combine,
        lax.all_gather(returned, "ctx", axis=1, tiled=True),
        preferred_element_type=jnp.float32,
    )
    return mixed.astype(jnp.bfloat16)


def solution(mesh):
    in_specs = (
        P("dp", "ctx", None),
        P(),
        P(("dp", "ctx"), None, None),
        P(("dp", "ctx"), None, None),
    )
    out_specs = P("dp", "ctx", None)
    return jax.shard_map(shards, mesh=mesh, in_specs=in_specs, out_specs=out_specs, check_vma=False)
```

profile of v0, /device:TPU:1, one launch (start us, length us, event | category | flops | bytes accessed | tf_op | source)
XLA Modules:
  0.0 80.7 jit_solution(9452041933624076778)
XLA Ops:
  0.0 1.0 %reshape.38 = bf16[1280,8,4,2]{0,3,2,1:T(2,128)(2,1)S(1)} reshape(bf16[1280,64]{0,1:T(8,128)(2,1)} %param.7) | data formatting | bytes 327680 | tf_op jit(solution)/shard_map/reshape | solution.py:42
  1.0 0.1 copy.22
  1.1 0.1 reshape.60
  1.2 5.0 %fusion.98 = (f32[4,64]{1,0:T(4,128)S(1)}, f32[4,640,64]{1,2,0:T(8,128)S(1)}) fusion(bf16[4,640,1280]{2,1,0:T(8,128)(2,1)} %param.6, bf16[1280,64,1]{0,1,2:T(8,128)(2,1)S(1)} %reshape.60), kind=kOutput, calls=%fused_computation.108 | convolution fusion | flops 419593984 | bytes 7373824 | tf_op jit(solution)/shard_map/ctd,dj->ctj/dot_general | solution.py:46
  6.2 0.3 fusion.34
  6.5 6.0 %all-gather.3 = f32[4,4,64]{2,1,0:T(4,128)S(1)} all-gather(f32[1,4,64]{2,1,0:T(4,128)S(1)} %bitcast.63), channel_id=3, replica_groups=mesh['dp'=8,'ctx'=4] {'ctx'}, dimensions={0}, use_global_device_ids=true | all-gather | bytes 5120 | tf_op jit(solution)/shard_map/all_gather | solution.py:8
  12.5 5.5 %all-gather.2 = f32[4,4,64]{2,1,0:T(4,128)S(1)} all-gather(f32[1,4,64]{2,1,0:T(4,128)S(1)} %bitcast.62), channel_id=2, replica_groups=mesh['dp'=8,'ctx'=4] {'ctx'}, dimensions={0}, use_global_device_ids=true | all-gather | bytes 5120 | tf_op jit(solution)/shard_map/all_gather | solution.py:8
  18.0 0.1 while.17
  18.1 0.2 divide_convert_fusion
  18.3 0.1 reshape.40
  18.4 4.1 %fusion.12 = bf16[4,8,4,2,1280]{4,1,3,2,0:T(8,128)(2,1)S(1)} fusion(bf16[4,640,1280]{2,1,0:T(8,128)(2,1)} %param.6, bf16[4,640,4,8,2]{1,4,3,2,0:T(2,128)(2,1)S(1)} %reshape.40), kind=kOutput, calls=%fused_computation.14 | convolution fusion | flops 419758080 | bytes 7536640 | tf_op jit(solution)/shard_map/ctabs,ctd->cbasd/dot_general | solution.py:58
  22.5 0.5 copy.30
  23.1 23.5 %all_to_all.10 = bf16[4,32,2,1280]{3,2,0,1:T(2,128)(2,1)S(1)} all-to-all(bf16[4,32,2,1280]{3,2,0,1:T(2,128)(2,1)S(1)} %bitcast.60), channel_id=1, replica_groups=mesh['dp'=8,'ctx'=4] {'dp','ctx'}, dimensions={1} | all-to-all | bytes 1310720 | tf_op jit(solution)/shard_map/all_to_all | solution.py:62
  46.6 0.7 bitcast_reduce_fusion
  47.3 0.1 copy.26
  47.4 0.1 convert_element_type.40
  47.5 8.0 %fusion.15 = bf16[64,1280]{1,0:T(8,128)(2,1)S(1)} fusion(bf16[1,2560,1280]{2,1,0:T(8,128)(2,1)} %param.9, bf16[64,1280]{1,0:T(8,128)(2,1)S(1)} %convert_element_type.40, bf16[1,1280,2560]{2,1,0:T(8,128)(2,1)} %param.8), kind=kOutput, calls=%fused_computation.15 | convolution fusion | flops 849592320 | bytes 13434880 | tf_op jit(solution)/shard_map/dot_general | solution.py:31
  55.5 0.1 reshape.44
  55.6 0.8 copy.27
  56.3 3.4 %all-to-all-start.1 = ((bf16[4,8,2,1280]{3,2,0,1:T(2,128)(2,1)}), bf16[4,8,2,1280]{3,2,0,1:T(2,128)(2,1)S(1)}, u32[]{:S(2)}, u32[]{:S(2)}) async-start(bf16[4,8,2,1280]{3,2,0,1:T(2,128)(2,1)} %copy.27), calls=%async_computation.1 | async-start | bytes 327680 | tf_op jit(solution)/shard_map/all_to_all | solution.py:66
  59.7 0.2 fusion.99
  59.9 6.3 %all-to-all-done.1 = bf16[4,8,2,1280]{3,2,0,1:T(2,128)(2,1)S(1)} async-done(((bf16[4,8,2,1280]{3,2,0,1:T(2,128)(2,1)}), bf16[4,8,2,1280]{3,2,0,1:T(2,128)(2,1)S(1)}, u32[]{:S(2)}, u32[]{:S(2)}) %all-to-all-start.1) | async-done | bytes 163872 | tf_op jit(solution)/shard_map/all_to_all | solution.py:66
  66.2 0.1 copy.28
  66.3 0.1 reshape.45
  66.4 9.7 %all_gather.19 = bf16[4,64,1280]{2,1,0:T(8,128)(2,1)S(1)} all-gather(bf16[4,16,1280]{2,1,0:T(8,128)(2,1)S(1)} %reshape.45), channel_id=1, replica_groups=mesh['dp'=8,'ctx'=4] {'ctx'}, dimensions={1}, use_global_device_ids=true | all-gather | bytes 819200 | tf_op jit(solution)/shard_map/all_gather | solution.py:71
  76.0 4.7 %convolution_convert_fusion = bf16[4,640,1280]{2,1,0:T(8,128)(2,1)} fusion(bf16[4,64,1280]{2,1,0:T(8,128)(2,1)S(1)} %all_gather.19, f32[4,640]{1,0:T(4,128)S(1)} %fusion.99, f32[4,640,64]{1,2,0:T(8,128)S(1)} %get-tuple-element.153), kind=kOutput, calls=%fused_computation.12 | convolution fusion | flops 423201344 | bytes 7874560 | tf_op jit(solution)/shard_map/ctj,cjd->ctd/dot_general | solution.py:68
  (6 shorter events, 0.1 us)
Async XLA Ops:
  56.3 9.8 %all-to-all-start.1 = ((bf16[4,8,2,1280]{3,2,0,1:T(2,128)(2,1)}), bf16[4,8,2,1280]{3,2,0,1:T(2,128)(2,1)S(1)}, u32[]{:S(2)}, u32[]{:S(2)}) async-start(bf16[4,8,2,1280]{3,2,0,1:T(2,128)(2,1)} %copy.27), calls=%async_computation.1 | async-start | bytes 327680 | tf_op jit(solution)/shard_map/all_to_all | solution.py:66
where the time goes:
time: 81.2 us; the launch traced here: 80.7 us
  blocking collectives  44.7 us (55%)
  matrix products  21.8 us (27%)
  waiting for transfers between devices  6.29 us (8%)
  starting transfers between devices  3.38 us (4%)
  local copies, waits for them, and re-layouts  3 us (4%)
  other arithmetic  1.36 us (2%)
    all_to_all x1, blocking collectives, shards(): lax.all_to_all(grouped, ('dp', 'ctx'), split_axis=1, concat_axis=1, tiled...  23.5 us
    all_gather x2, blocking collectives, merged(): everything = jax.tree.map(lambda part: lax.all_gather(part, axis), x)  11.5 us
    all_gather x1, blocking collectives, shards(): lax.all_gather(returned, 'ctx', axis=1, tiled=True)  9.66 us
    dot_general x1, matrix products, expert_rows(): jnp.dot(hidden, down_matrix, preferred_element_type=jnp.float32)  8.01 us
    all_to_all x1, waiting for transfers between devices, shards(): lax.all_to_all(results, 'dp', split_axis=1, concat_axis=1, tiled=True)  6.29 us
    dot_general x1, matrix products, shards(): jnp.einsum('ctd,dj->ctj', tokens, ordered, preferred_element_type=jnp.flo...  5.03 us
    dot_general x1, matrix products, shards(): jnp.einsum('ctj,cjd->ctd', combine, lax.all_gather(returned, 'ctx', axis=...  4.72 us
    dot_general x1, matrix products, shards(): jnp.einsum('ctabs,ctd->cbasd', split_dispatch, tokens, preferred_element_...  4.08 us
  transfers between devices with their start and end apart: 1, of which 1 were waited for; matrix products, arithmetic and copies ran while one was open for 0% of the time, Pallas kernels for 0%

commit v1 on v0

v1 whole, which is shorter than its diff:
```python
import functools

import jax
import jax.numpy as jnp
import numpy as np
from jax import lax
from jax.experimental import pallas as pl
from jax.experimental.pallas import tpu as pltpu
from jax.sharding import PartitionSpec as P

MESH = pl.DeviceIdType.MESH
CORES = 2
F32 = jnp.float32
BF16 = jnp.bfloat16


def clip_rows(shape, clip, per_clip, group):
    place = lax.rem(lax.broadcasted_iota(jnp.int32, shape, 0), group)
    return (place >= clip * per_clip) & (place < (clip + 1) * per_clip)


def exchange(
    dims, tok_hbm, router_ref, spread_ref, up_hbm, down_hbm, gathered_ref, combine_ref,
    tok, up, down, logit, diag, acc, part, from_core, chip, from_y, slab, rows_in, result, pool,
    stat, stats_in,
    tok_sem, weight_sem, stat_sem, core_sem, y_sem, dp_sem, back_sem, ysend_sem, csend_sem,
):
    n_dp, n_ctx, clips, tok_dev, per_expert, chunks, width = dims
    n_y = n_ctx // CORES
    group = clips * per_expert
    rows = n_dp * n_ctx * group
    dp = lax.axis_index("dp")
    ctx = lax.axis_index("ctx")
    y = ctx // CORES
    core = ctx % CORES
    other = 1 - core

    token_copies = []
    for c in range(clips):
        copy = pltpu.make_async_copy(tok_hbm.at[c], tok.at[pl.ds(c * tok_dev, tok_dev)], tok_sem.at[c])
        copy.start()
        token_copies.append(copy)
    up_copy = pltpu.make_async_copy(up_hbm.at[0], up, weight_sem.at[0])
    up_copy.start()
    down_copy = pltpu.make_async_copy(down_hbm.at[0], down, weight_sem.at[1])
    down_copy.start()

    barrier = pltpu.get_barrier_semaphore()
    for k in range(1, n_ctx):
        pl.semaphore_signal(barrier, inc=1, device_id=(dp, (ctx + k) % n_ctx), device_id_type=MESH)
    for k in range(1, n_dp):
        pl.semaphore_signal(barrier, inc=1, device_id=((dp + k) % n_dp, ctx), device_id_type=MESH)

    def send(src, dst, sems, index, target):
        copy = pltpu.make_async_remote_copy(
            src_ref=src, dst_ref=dst, send_sem=sems.at[(0,) + index], recv_sem=sems.at[(1,) + index],
            device_id=target, device_id_type=MESH,
        )
        copy.start()
        return copy

    routed = jnp.dot(spread_ref[...], router_ref[...], preferred_element_type=F32).astype(BF16)
    for c in range(clips):
        token_copies[c].wait()
        here = lax.dot_general(
            routed, tok[pl.ds(c * tok_dev, tok_dev), :], (((1,), (1,)), ((), ())), preferred_element_type=F32
        )
        if c == 0:
            logit[...] = here
        else:
            logit[...] = jnp.where(clip_rows((rows, tok_dev), c, per_expert, group), here, logit[...])
    highest = jnp.max(logit[...], axis=1, keepdims=True)
    powers = jnp.exp(logit[...] - highest)
    total = jnp.sum(powers, axis=1, keepdims=True)
    lane = lax.broadcasted_iota(jnp.int32, (rows, 128), 1)
    stat[...] = jnp.where(lane == 0, highest, total).T[0:8, :]
    pl.semaphore_wait(barrier, n_ctx - 1 + n_dp - 1)
    stat_copies = [
        send(stat, stats_in.at[k - 1], stat_sem, (k - 1,), (dp, (ctx + k) % n_ctx)) for k in range(1, n_ctx)
    ]
    for c in range(clips):
        diag[:, pl.ds(c * tok_dev, tok_dev)] = jnp.where(
            clip_rows((rows, tok_dev), c, per_expert, group), powers, 0.0
        ).astype(BF16)

    started = []

    def block_sums(f):
        return jnp.dot(diag[...], tok[:, pl.ds(f * width, width)], preferred_element_type=F32)

    def first(f, value, scale):
        value = (value * scale).reshape(CORES, n_y, n_dp, group, width)
        part[f] = value.astype(BF16)
        copy = send(part.at[f, other], from_core.at[f], core_sem, (f,), (dp, y * CORES + other))
        return copy

    def second(f, copy):
        copy.wait_recv()
        chip[f] = (part[f, core].astype(F32) + from_core[f].astype(F32)).astype(BF16)
        copies = []
        for k in range(1, n_y):
            there = (y + k) % n_y
            copies.append(
                send(chip.at[f, there], from_y.at[f, k - 1], y_sem, (f, k - 1), (dp, there * CORES + core))
            )
        return copies

    def third(f, copies):
        value = chip[f, y].astype(F32)
        for k in range(1, n_y):
            copies[k - 1].wait_recv()
            value = value + from_y[f, k - 1].astype(F32)
        slab[f] = value.astype(BF16)
        rows_in[f, dp] = slab[f, dp]
        return [
            send(slab.at[f, (dp + k) % n_dp], rows_in.at[f, dp], dp_sem, (f, k - 1), ((dp + k) % n_dp, ctx))
            for k in range(1, n_dp)
        ]

    def fourth(f, copies):
        for copy in copies:
            copy.wait_recv()
        value = rows_in[f].astype(F32).reshape(n_dp * group, width).astype(BF16)
        term = jnp.dot(value, up[pl.ds(f * width, width), :], preferred_element_type=F32)
        acc[...] = term if f == 0 else acc[...] + term

    opening = block_sums(0)
    for copy in stat_copies:
        copy.wait_recv()
    best, amount = stat[0:1, :], stat[1:2, :]
    top = best
    for k in range(1, n_ctx):
        top = jnp.maximum(top, stats_in[k - 1, 0:1, :])
    whole = amount * jnp.exp(best - top)
    for k in range(1, n_ctx):
        whole = whole + stats_in[k - 1, 1:2, :] * jnp.exp(stats_in[k - 1, 0:1, :] - top)
    scale = jnp.broadcast_to(jnp.exp(best - top) / whole, (128, rows)).T[:, 0:1]

    one, two, three = {}, {}, {}
    for t in range(chunks + 2):
        if t < chunks:
            one[t] = first(t, opening if t == 0 else block_sums(t), scale)
        if 0 <= t - 1 < chunks:
            two[t - 1] = second(t - 1, one[t - 1])
        if 0 <= t - 2 < chunks:
            three[t - 2] = third(t - 2, two[t - 2])

    blocks = logit[...].reshape(rows // group, group, tok_dev)
    peak = jnp.max(blocks, axis=0)

    def over_slots(values, reduce, neutral):
        out = values
        for c in range(clips):
            mine = clip_rows((group, tok_dev), c, per_expert, group)
            out = jnp.where(mine, reduce(jnp.where(mine, values, neutral), axis=0, keepdims=True), out)
        return out

    peak = over_slots(peak, jnp.max, -jnp.inf)
    powers = jnp.exp(blocks - peak[None])
    norm = over_slots(jnp.sum(powers, axis=0), jnp.sum, 0.0)
    combine_ref[...] = (powers / norm[None]).reshape(rows, tok_dev).astype(BF16)

    up_copy.wait()
    for f in range(chunks):
        fourth(f, three[f])
    value = acc[...]
    hidden = (0.5 * value * (1.0 + lax.erf(value * np.float32(np.sqrt(0.5))))).astype(BF16)
    down_copy.wait()

    def fifth(f):
        value = jnp.dot(hidden, down[:, pl.ds(f * width, width)], preferred_element_type=F32)
        result[f] = value.reshape(n_dp, group, width).astype(BF16)
        pool[f, core, y, dp] = result[f, dp]
        return [
            send(
                result.at[f, (dp + k) % n_dp], pool.at[f, core, y, dp], back_sem, (f, k - 1),
                ((dp + k) % n_dp, ctx),
            )
            for k in range(1, n_dp)
        ]

    def sixth(f, copies):
        for copy in copies:
            copy.wait_recv()
        piece = pool.at[f, core, y]
        beyond = [
            send(piece, piece, ysend_sem, (f, k - 1), (dp, ((y + k) % n_y) * CORES + core)) for k in range(1, n_y)
        ]
        across = [send(piece, piece, csend_sem, (f, 0), (dp, y * CORES + other))]
        return beyond, across

    def seventh(f, copies):
        beyond, across = copies
        for k in range(1, n_y):
            beyond[k - 1].wait_recv()
            piece = pool.at[f, core, (y + n_y - k) % n_y]
            across.append(send(piece, piece, csend_sem, (f, k), (dp, y * CORES + other)))
        return across

    five, six, seven = {}, {}, {}
    for t in range(chunks + 2):
        if t < chunks:
            five[t] = fifth(t)
        if 0 <= t - 1 < chunks:
            six[t - 1] = sixth(t - 1, five[t - 1])
        if 0 <= t - 2 < chunks:
            seven[t - 2] = seventh(t - 2, six[t - 2])
    for f in range(chunks):
        for copy in seven[f]:
            copy.wait_recv()
        gathered_ref[f] = pool[f].astype(F32).reshape(rows, width).astype(BF16)

    for copy in stat_copies:
        copy.wait_send()
    for f in range(chunks):
        for copy in [one[f]] + two[f] + three[f] + five[f] + six[f][0] + seven[f]:
            copy.wait_send()


def mix(clips, per_expert, chunks, width, combine_ref, gathered_ref, out_ref):
    group = clips * per_expert
    mine = clip_rows(combine_ref.shape, pl.program_id(0), per_expert, group)
    weights = jnp.where(mine, combine_ref[...].astype(F32), 0.0).T.astype(BF16)
    for f in range(chunks):
        out_ref[0, :, pl.ds(f * width, width)] = jnp.dot(
            weights, gathered_ref[f], preferred_element_type=F32
        ).astype(BF16)


def shards(n_dp, n_ctx, tokens, router, expert_up, expert_down):
    clips, tok_dev, feature = tokens.shape
    slots = router.shape[1]
    hidden = expert_up.shape[2]
    per_expert = slots // (n_dp * n_ctx)
    n_y = n_ctx // CORES
    group = clips * per_expert
    rows = n_dp * n_ctx * group
    width = 256
    chunks = feature // width
    order = np.arange(slots).reshape(n_dp, n_y, CORES, 1, per_expert).transpose(2, 1, 0, 3, 4)
    order = np.broadcast_to(order, (CORES, n_y, n_dp, clips, per_expert)).reshape(-1)
    spread = jnp.asarray(order[:, None] == np.arange(slots)[None, :], BF16)
    dims = (n_dp, n_ctx, clips, tok_dev, per_expert, chunks, width)
    vmem = pl.BlockSpec(memory_space=pltpu.VMEM)
    hbm = pl.BlockSpec(memory_space=pl.ANY)
    piece = (n_dp, group, width)
    dma = pltpu.SemaphoreType.DMA
    gathered, combine = pl.pallas_call(
        functools.partial(exchange, dims),
        out_shape=(
            jax.ShapeDtypeStruct((chunks, rows, width), BF16),
            jax.ShapeDtypeStruct((rows, tok_dev), BF16),
        ),
        in_specs=[hbm, vmem, vmem, hbm, hbm],
        out_specs=(vmem, vmem),
        scratch_shapes=[
            pltpu.VMEM((clips * tok_dev, feature), BF16),
            pltpu.VMEM((feature, hidden), BF16),
            pltpu.VMEM((hidden, feature), BF16),
            pltpu.VMEM((rows, tok_dev), F32),
            pltpu.VMEM((rows, clips * tok_dev), BF16),
            pltpu.VMEM((n_dp * group, hidden), F32),
            pltpu.VMEM((chunks, CORES, n_y) + piece, BF16),
            pltpu.VMEM((chunks, n_y) + piece, BF16),
            pltpu.VMEM((chunks, n_y) + piece, BF16),
            pltpu.VMEM((chunks, n_y - 1) + piece, BF16),
            pltpu.VMEM((chunks,) + piece, BF16),
            pltpu.VMEM((chunks,) + piece, BF16),
            pltpu.VMEM((chunks,) + piece, BF16),
            pltpu.VMEM((chunks, CORES, n_y) + piece, BF16),
            pltpu.VMEM((8, rows), F32),
            pltpu.VMEM((n_ctx - 1, 8, rows), F32),
            dma((clips,)),
            dma((2,)),
            dma((2, n_ctx - 1)),
            dma((2, chunks)),
            dma((2, chunks, n_y - 1)),
            dma((2, chunks, n_dp - 1)),
            dma((2, chunks, n_dp - 1)),
            dma((2, chunks, n_y - 1)),
            dma((2, chunks, n_y)),
        ],
        compiler_params=pltpu.CompilerParams(collective_id=0, has_side_effects=True),
        name="exchange",
    )(tokens, router.T, spread, expert_up, expert_down)
    return pl.pallas_call(
        functools.partial(mix, clips, per_expert, chunks, width),
        grid=(clips,),
        out_shape=jax.ShapeDtypeStruct(tokens.shape, BF16),
        in_specs=[
            pl.BlockSpec((rows, tok_dev), lambda c: (0, 0)),
            pl.BlockSpec((chunks, rows, width), lambda c: (0, 0, 0)),
        ],
        out_specs=pl.BlockSpec((1, tok_dev, feature), lambda c: (c, 0, 0)),
        name="mix",
    )(combine, gathered)


def solution(mesh):
    in_specs = (
        P("dp", "ctx", None),
        P(),
        P(("dp", "ctx"), None, None),
        P(("dp", "ctx"), None, None),
    )
    out_specs = P("dp", "ctx", None)
    body = functools.partial(shards, mesh.shape["dp"], mesh.shape["ctx"])
    return jax.shard_map(body, mesh=mesh, in_specs=in_specs, out_specs=out_specs, check_vma=False)
```

time: 81.2 us -> 53.6 us (0.66)
  Pallas kernels: 0 us -> 53.4 us
  blocking collectives: 44.7 us -> 0 us
  matrix products: 21.8 us -> 0 us
  waiting for transfers between devices: 6.29 us -> 0 us
  starting transfers between devices: 3.38 us -> 0 us
  local copies, waits for them, and re-layouts: 3 us -> 0 us
  other arithmetic: 1.36 us -> 0 us
    pallas_call x0 -> x2, Pallas kernels: none -> 53.4 us  [the longest x1 47.9 us: shards(): pl.pallas_call(functools.partial(exchange, dims), out_shape=(jax.ShapeDty...]
    all_to_all x1 -> x0, blocking collectives: 23.5 us -> none  [shards(): lax.all_to_all(grouped, ('dp', 'ctx'), split_axis=1, concat_axis=1, tiled...]
    dot_general x4 -> x0, matrix products: 21.8 us -> none  [the longest x1 8.01 us: expert_rows(): jnp.dot(hidden, down_matrix, preferred_element_type=jnp.float32)]
    all_gather x3 -> x0, blocking collectives: 21.2 us -> none  [the longest x2 11.5 us: merged(): everything = jax.tree.map(lambda part: lax.all_gather(part, axis), x)]
    all_to_all x1 -> x0, waiting for transfers between devices: 6.29 us -> none  [shards(): lax.all_to_all(results, 'dp', split_axis=1, concat_axis=1, tiled=True)]
    all_to_all x1 -> x0, starting transfers between devices: 3.38 us -> none  [shards(): lax.all_to_all(results, 'dp', split_axis=1, concat_axis=1, tiled=True)]
    reshape x7 -> x0, local copies, waits for them, and re-layouts: 2.59 us -> none  [the longest x1 0.98 us: shards(): router.reshape(feature, dp_size, ctx_size, per_expert).transpose(0, 2, 1, 3)]
    reduce_sum x2 -> x0, other arithmetic: 0.93 us -> none  [the longest x1 0.67 us: shards(): jnp.sum(blocks, axis=2).astype(jnp.bfloat16)]
  transfers between devices with their start and end apart: 1 -> 0, of which waited for: 1 -> 0; matrix products, arithmetic and copies ran while one was open for 0% -> 0% of each run, Pallas kernels for 0% -> 0%
where the time goes in v1:
time: 53.6 us; the launch traced here: 53.4 us
  Pallas kernels  53.4 us (100%)
    pallas_call x1, Pallas kernels, shards(): pl.pallas_call(functools.partial(exchange, dims), out_shape=(jax.ShapeDty...  47.9 us
    pallas_call x1, Pallas kernels, shards(): pl.pallas_call(functools.partial(mix, clips, per_expert, chunks, width),...  5.55 us

profile of v1, /device:TPU:1, one launch (start us, length us, event | category | flops | bytes accessed | tf_op | source)
XLA Modules:
  0.0 53.4 jit_solution(17977081500696528499)
XLA Ops:
  0.0 47.9 %exchange.1 = (bf16[5,256,256]{2,1,0:T(8,128)(2,1)}, bf16[256,640]{1,0:T(8,128)(2,1)}) custom-call(bf16[4,640,1280]{2,1,0:T(8,128)(2,1)} %tok_hbm.1, bf16[64,1280]{1,0:T(8,128)(2,1)} %bitcast.1, bf16[256,64]{1,0:T(8,128)(2,1)} %constant.2.clone.spread_ref, bf16[1,1280,2560]{2,1,0:T(8,128)(2,1)} %up_hbm.1, bf16[1,2560,1280]{2,1,0:T(8,128)(2,1)} %down_hbm.1), custom_call_target="tpu_custom_call" | custom-call | tf_op jit(solution)/shard_map/exchange/pallas_call | solution.py:248
  47.9 5.5 %mix.1 = bf16[4,640,1280]{2,1,0:T(8,128)(2,1)} custom-call(bf16[256,640]{1,0:T(8,128)(2,1)} %get-tuple-element.7.combine_ref, bf16[5,256,256]{2,1,0:T(8,128)(2,1)} %get-tuple-element.8.gathered_ref), custom_call_target="tpu_custom_call" | custom-call | tf_op jit(solution)/shard_map/mix/pallas_call | solution.py:286

commit v2 on v1

--- a/solution.py
+++ b/solution.py
@@ -10,18 +10,19 @@
 
 MESH = pl.DeviceIdType.MESH
 CORES = 2
+LAG = 4
 F32 = jnp.float32
 BF16 = jnp.bfloat16
 
 
-def clip_rows(shape, clip, per_clip, group):
-    place = lax.rem(lax.broadcasted_iota(jnp.int32, shape, 0), group)
+def clip_rows(shape, clip, per_clip, group, dim=0):
+    place = lax.rem(lax.broadcasted_iota(jnp.int32, shape, dim), group)
     return (place >= clip * per_clip) & (place < (clip + 1) * per_clip)
 
 
 def exchange(
     dims, tok_hbm, router_ref, spread_ref, up_hbm, down_hbm, gathered_ref, combine_ref,
-    tok, up, down, logit, diag, acc, part, from_core, chip, from_y, slab, rows_in, result, pool,
+    tok, up, down, flipped, logit, diag, sums, acc, part, from_core, chip, from_y, slab, rows_in, result, pool,
     stat, stats_in,
     tok_sem, weight_sem, stat_sem, core_sem, y_sem, dp_sem, back_sem, ysend_sem, csend_sem,
 ):
@@ -59,16 +60,15 @@
         copy.start()
         return copy
 
-    routed = jnp.dot(spread_ref[...], router_ref[...], preferred_element_type=F32).astype(BF16)
+    routed = jnp.dot(spread_ref[...], router_ref[...], preferred_element_type=F32).T.astype(BF16)
     for c in range(clips):
         token_copies[c].wait()
-        here = lax.dot_general(
-            routed, tok[pl.ds(c * tok_dev, tok_dev), :], (((1,), (1,)), ((), ())), preferred_element_type=F32
-        )
+        here = jnp.dot(tok[pl.ds(c * tok_dev, tok_dev), :], routed, preferred_element_type=F32)
         if c == 0:
-            logit[...] = here
+            flipped[...] = here
         else:
-            logit[...] = jnp.where(clip_rows((rows, tok_dev), c, per_expert, group), here, logit[...])
+            flipped[...] = jnp.where(clip_rows((tok_dev, rows), c, per_expert, group, 1), here, flipped[...])
+    logit[...] = flipped[...].T
     highest = jnp.max(logit[...], axis=1, keepdims=True)
     powers = jnp.exp(logit[...] - highest)
     total = jnp.sum(powers, axis=1, keepdims=True)
@@ -83,8 +83,6 @@
             clip_rows((rows, tok_dev), c, per_expert, group), powers, 0.0
         ).astype(BF16)
 
-    started = []
-
     def block_sums(f):
         return jnp.dot(diag[...], tok[:, pl.ds(f * width, width)], preferred_element_type=F32)
 
@@ -124,7 +122,8 @@
         term = jnp.dot(value, up[pl.ds(f * width, width), :], preferred_element_type=F32)
         acc[...] = term if f == 0 else acc[...] + term
 
-    opening = block_sums(0)
+    for f in range(chunks):
+        sums[f] = block_sums(f)
     for copy in stat_copies:
         copy.wait_recv()
     best, amount = stat[0:1, :], stat[1:2, :]
@@ -137,13 +136,13 @@
     scale = jnp.broadcast_to(jnp.exp(best - top) / whole, (128, rows)).T[:, 0:1]
 
     one, two, three = {}, {}, {}
-    for t in range(chunks + 2):
+    for t in range(chunks + LAG):
         if t < chunks:
-            one[t] = first(t, opening if t == 0 else block_sums(t), scale)
+            one[t] = first(t, sums[t], scale)
         if 0 <= t - 1 < chunks:
             two[t - 1] = second(t - 1, one[t - 1])
-        if 0 <= t - 2 < chunks:
-            three[t - 2] = third(t - 2, two[t - 2])
+        if 0 <= t - LAG < chunks:
+            three[t - LAG] = third(t - LAG, two[t - LAG])
 
     blocks = logit[...].reshape(rows // group, group, tok_dev)
     peak = jnp.max(blocks, axis=0)
@@ -158,7 +157,7 @@
     peak = over_slots(peak, jnp.max, -jnp.inf)
     powers = jnp.exp(blocks - peak[None])
     norm = over_slots(jnp.sum(powers, axis=0), jnp.sum, 0.0)
-    combine_ref[...] = (powers / norm[None]).reshape(rows, tok_dev).astype(BF16)
+    combine_ref[...] = (powers / norm[None]).reshape(rows, tok_dev).T.astype(BF16)
 
     up_copy.wait()
     for f in range(chunks):
@@ -198,11 +197,11 @@
         return across
 
     five, six, seven = {}, {}, {}
+    for t in range(chunks):
+        five[t] = fifth(t)
     for t in range(chunks + 2):
         if t < chunks:
-            five[t] = fifth(t)
-        if 0 <= t - 1 < chunks:
-            six[t - 1] = sixth(t - 1, five[t - 1])
+            six[t] = sixth(t, five[t])
         if 0 <= t - 2 < chunks:
             seven[t - 2] = seventh(t - 2, six[t - 2])
     for f in range(chunks):
@@ -219,8 +218,8 @@
 
 def mix(clips, per_expert, chunks, width, combine_ref, gathered_ref, out_ref):
     group = clips * per_expert
-    mine = clip_rows(combine_ref.shape, pl.program_id(0), per_expert, group)
-    weights = jnp.where(mine, combine_ref[...].astype(F32), 0.0).T.astype(BF16)
+    mine = clip_rows(combine_ref.shape, pl.program_id(0), per_expert, group, 1)
+    weights = jnp.where(mine, combine_ref[...].astype(F32), 0.0).astype(BF16)
     for f in range(chunks):
         out_ref[0, :, pl.ds(f * width, width)] = jnp.dot(
             weights, gathered_ref[f], preferred_element_type=F32
@@ -236,6 +235,7 @@
     group = clips * per_expert
     rows = n_dp * n_ctx * group
     width = 256
+    parts = 1
     chunks = feature // width
     order = np.arange(slots).reshape(n_dp, n_y, CORES, 1, per_expert).transpose(2, 1, 0, 3, 4)
     order = np.broadcast_to(order, (CORES, n_y, n_dp, clips, per_expert)).reshape(-1)
@@ -249,7 +249,7 @@
         functools.partial(exchange, dims),
         out_shape=(
             jax.ShapeDtypeStruct((chunks, rows, width), BF16),
-            jax.ShapeDtypeStruct((rows, tok_dev), BF16),
+            jax.ShapeDtypeStruct((tok_dev, rows), BF16),
         ),
         in_specs=[hbm, vmem, vmem, hbm, hbm],
         out_specs=(vmem, vmem),
@@ -257,8 +257,10 @@
             pltpu.VMEM((clips * tok_dev, feature), BF16),
             pltpu.VMEM((feature, hidden), BF16),
             pltpu.VMEM((hidden, feature), BF16),
+            pltpu.VMEM((tok_dev, rows), F32),
             pltpu.VMEM((rows, tok_dev), F32),
             pltpu.VMEM((rows, clips * tok_dev), BF16),
+            pltpu.VMEM((chunks, rows, width), F32),
             pltpu.VMEM((n_dp * group, hidden), F32),
             pltpu.VMEM((chunks, CORES, n_y) + piece, BF16),
             pltpu.VMEM((chunks, n_y) + piece, BF16),
@@ -285,13 +287,13 @@
     )(tokens, router.T, spread, expert_up, expert_down)
     return pl.pallas_call(
         functools.partial(mix, clips, per_expert, chunks, width),
-        grid=(clips,),
+        grid=(clips, parts),
         out_shape=jax.ShapeDtypeStruct(tokens.shape, BF16),
         in_specs=[
-            pl.BlockSpec((rows, tok_dev), lambda c: (0, 0)),
-            pl.BlockSpec((chunks, rows, width), lambda c: (0, 0, 0)),
+            pl.BlockSpec((tok_dev // parts, rows), lambda c, t: (t, 0)),
+            pl.BlockSpec((chunks, rows, width), lambda c, t: (0, 0, 0)),
         ],
-        out_specs=pl.BlockSpec((1, tok_dev, feature), lambda c: (c, 0, 0)),
+        out_specs=pl.BlockSpec((1, tok_dev // parts, feature), lambda c, t: (c, t, 0)),
         name="mix",
     )(combine, gathered)
 

time: 53.6 us -> 44.7 us (0.83)
  Pallas kernels: 53.4 us -> 44.6 us
    pallas_call x1, Pallas kernels: 47.9 us -> 39.2 us  [shards(): pl.pallas_call(functools.partial(exchange, dims), out_shape=(jax.ShapeDty...]
where the time goes in v2:
time: 44.7 us; the launch traced here: 44.6 us
  Pallas kernels  44.6 us (100%)
    pallas_call x1, Pallas kernels, shards(): pl.pallas_call(functools.partial(exchange, dims), out_shape=(jax.ShapeDty...  39.2 us
    pallas_call x1, Pallas kernels, shards(): pl.pallas_call(functools.partial(mix, clips, per_expert, chunks, width),...  5.34 us

profile of v2, /device:TPU:1, one launch (start us, length us, event | category | flops | bytes accessed | tf_op | source)
XLA Modules:
  0.0 44.6 jit_solution(12203260624997776166)
XLA Ops:
  0.0 39.2 %exchange.1 = (bf16[5,256,256]{2,1,0:T(8,128)(2,1)}, bf16[640,256]{1,0:T(8,128)(2,1)}) custom-call(bf16[4,640,1280]{2,1,0:T(8,128)(2,1)} %tok_hbm.1, bf16[64,1280]{1,0:T(8,128)(2,1)} %bitcast.1, bf16[256,64]{1,0:T(8,128)(2,1)} %constant.2.clone.spread_ref, bf16[1,1280,2560]{2,1,0:T(8,128)(2,1)} %up_hbm.1, bf16[1,2560,1280]{2,1,0:T(8,128)(2,1)} %down_hbm.1), custom_call_target="tpu_custom_call" | custom-call | tf_op jit(solution)/shard_map/exchange/pallas_call | solution.py:248
  39.2 5.3 %mix.1 = bf16[4,640,1280]{2,1,0:T(8,128)(2,1)} custom-call(bf16[640,256]{1,0:T(8,128)(2,1)} %get-tuple-element.7.combine_ref, bf16[5,256,256]{2,1,0:T(8,128)(2,1)} %get-tuple-element.8.gathered_ref), custom_call_target="tpu_custom_call" | custom-call | tf_op jit(solution)/shard_map/mix/pallas_call | solution.py:288
